TPU v7x, 32 devices: a whole 2x2x4 slice. The times are simulated.
32 devices in a mesh: ctx: 8 (over z, y), head: 4 (over x, core).
Axes of the slice: x: 2, y: 2, z: 4, core: 2. Of those that a mesh axis runs over, the one named last changes fastest.
Arguments:
- queries: bfloat16 [4096, 2048], P(('ctx', 'head')), may hold values from -6 to 6
- key_rows: bfloat16 [4096, 256], P(('ctx', 'head')), may hold values from -6 to 6
- value_rows: bfloat16 [4096, 256], P(('ctx', 'head')), may hold values from -8 to 8
- group_kv_head: int32 [4], replicated, may hold values from 0 to 1, as said below
- doc_ids: int32 [4096], replicated, may hold values from 0 to 127, never falling along the last dimension, each value on 1 to 64 neighbouring positions
Outputs:
- attended: bfloat16 [4096, 2048], P(('ctx', 'head'))
Inputs may be any that keep to these rules, and one draw needn't show every extreme that they name: `group_kv_head`: each key-value head is named by exactly two groups. `doc_ids`: ids never fall along the sequence and every id appears; a document holds at most 64 tokens, and one holds exactly that many.
All inputs are finite; a program needn't handle non-finite values.
Results may differ from a plain program's by a relative error of at most 0.0027.
Values may be sent and summed in bfloat16 or wider, within the bound.
No kernel may reach another device: no remote copies, remote signals or barrier semaphores. Data moves between devices by JAX's collectives and lax.ppermute only.
A program may use at most 64 MiB of HBM per device.

v0:
```python
import functools
import math

import jax
import jax.numpy as jnp
from jax import lax
from jax.experimental import pallas as pl
from jax.experimental.pallas import tpu as pltpu
from jax.sharding import PartitionSpec as P


HEAD_DIM = 128
HEADS_DEV = 4
WIDTH = HEADS_DEV * HEAD_DIM
AXES = ("ctx", "head")
neg_fill = -1e30
FACTOR = math.log2(math.e) / math.sqrt(HEAD_DIM)


def flat_index():
    return lax.axis_index("ctx") * lax.axis_size("head") + lax.axis_index("head")


def bias_of(visible):
    return jnp.where(visible, 0.0, neg_fill)


def scores_of(query, key, bias):
    raw = lax.dot_general(query, key, (((1,), (1,)), ((), ())), preferred_element_type=jnp.float32)
    return raw * FACTOR + jnp.concatenate([bias] * HEADS_DEV, axis=0)


def tall_scores(query, key, bias):
    raw = lax.dot_general(key, query, (((1,), (1,)), ((), ())), preferred_element_type=jnp.float32)
    return raw * FACTOR + bias


def softmax_parts(scores):
    expo = jnp.exp2(scores - jnp.max(scores, axis=1, keepdims=True))
    inverse = 1.0 / jnp.sum(expo, axis=1, keepdims=True)
    return expo.astype(jnp.bfloat16), inverse


def mix(weights, inverse, value):
    return (jnp.dot(weights, value, preferred_element_type=jnp.float32) * inverse).astype(jnp.bfloat16)


def column_of(row):
    return jnp.transpose(jnp.broadcast_to(row, (row.shape[1], row.shape[1])))


def head_stack(ref, g):
    return jnp.concatenate(
        [ref[:, g * WIDTH + h * HEAD_DIM:g * WIDTH + (h + 1) * HEAD_DIM] for h in range(HEADS_DEV)], axis=0)


def store_heads(ref, g, result):
    n = result.shape[0] // HEADS_DEV
    for h in range(HEADS_DEV):
        ref[:, g * WIDTH + h * HEAD_DIM:g * WIDTH + (h + 1) * HEAD_DIM] = result[h * n:(h + 1) * n]


def send_out(buf, out_ref, first, g, sem):
    cols = pl.ds(g * WIDTH, WIDTH)
    return pltpu.make_async_copy(buf.at[:, cols], out_ref.at[pl.ds(first, buf.shape[0]), cols], sem.at[g])


def columns(group_ref, g, offset=0):
    late, early = group_ref
    return pl.ds(pl.multiple_of(jnp.where(first_pair(), early[g], late[g]) * HEAD_DIM + offset, HEAD_DIM), HEAD_DIM)


def run_all(pairs, sem):
    copies = [pltpu.make_async_copy(a, b, sem.at[i]) for i, (a, b) in enumerate(pairs)]
    for copy in copies:
        copy.start()
    for copy in copies:
        copy.wait()


def first_pair():
    return flat_index() < 2


def last_rows(hbm, near):
    return hbm.at[pl.ds(hbm.shape[0] - near, near)]


def own_loads(doc_hbm, q_hbm, k_hbm, v_hbm, edge_ref, doc_ref, q_ref, k_ref, v_ref):
    near, width = edge_ref.shape[0], k_hbm.shape[1]
    return [(last_rows(k_hbm, near), edge_ref.at[:, pl.ds(0, width)]), (last_rows(v_hbm, near), edge_ref.at[:, pl.ds(width, width)]),
            (doc_hbm, doc_ref), (k_hbm, k_ref), (v_hbm, v_ref), (q_hbm, q_ref)]


def edge_kernel(group_hbm, doc_hbm, q_hbm, k_hbm, v_hbm, key_ref, value_ref, group_ref, *refs):
    *refs, sem = refs
    near = key_ref.shape[0]
    pairs = [(last_rows(k_hbm, near), key_ref), (last_rows(v_hbm, near), value_ref)]

    me = flat_index()

    @pl.when((me % 2 == 1) | (me == 0))
    def _():
        copies = [pltpu.make_async_copy(a, b, sem.at[i]) for i, (a, b) in enumerate(pairs)]
        for copy in copies:
            copy.start()

        @pl.when(first_pair())
        def _():
            run_all([(group_hbm, group_ref)] + own_loads(doc_hbm, q_hbm, k_hbm, v_hbm, *refs), sem.at[pl.ds(len(pairs), 7)])

        for copy in copies:
            copy.wait()


def load_kernel(given, group_hbm, doc_hbm, q_hbm, k_hbm, v_hbm, *refs):
    group_ref, *refs, sem = refs[given:]
    loads = [(group_hbm, group_ref)] + own_loads(doc_hbm, q_hbm, k_hbm, v_hbm, *refs)
    if not given:
        run_all(loads, sem)
        return

    @pl.when(jnp.logical_not(first_pair()))
    def _():
        run_all(loads, sem)


def inner_kernel(near, hops, group_ref, other_ref, doc_ref, q_ref, k_ref, v_ref, bias_ref, *out_ref):
    rows, width = q_ref.shape
    me = flat_index()
    own = doc_ref[pl.ds(me, 1), :]
    before = [doc_ref[pl.ds(jnp.maximum(me - j, 0), 1), :] for j in range(1, hops + 1)]
    col = column_of(own)
    t = lax.broadcasted_iota(jnp.int32, (rows, rows), 0)
    u = lax.broadcasted_iota(jnp.int32, (rows, rows), 1)
    if near == rows:
        seen = [(col == own) & (t <= u)]
        seen += [(column_of(before[j]) == own) & (t + (me - 1 - j) * rows >= 0) for j in range(hops)]
        seen = [bias_of(part) for part in seen]
    else:
        docs = column_of(jnp.where(lax.broadcasted_iota(jnp.int32, own.shape, 1) < near, own, before[0]))
        pos = jnp.where(t < near, t, t - rows)
        seen = [bias_of((docs == own) & (pos <= u) & (pos + me * rows >= 0))[:, :near]]
    bias_ref[...] = jnp.concatenate([jnp.concatenate(seen, axis=0)] * HEADS_DEV, axis=1)
    if near < rows:
        bias = bias_of((own == col) & (u <= t))[near:]
        far = q_ref.at[pl.ds(near, rows - near)]
        for g in range(width // WIDTH):
            c = columns((group_ref, other_ref), g)
            scores = scores_of(head_stack(far, g), k_ref[:, c], bias)
            store_heads(out_ref[0], g, mix(*softmax_parts(scores), v_ref[:, c]))


def with_rim(own_ref, near, rims, small, group_ref, g, offset):
    here = columns(group_ref, g)
    if small:
        me = flat_index()
        main, side = rims
        parts = [jnp.where((me % 2 == 1) | (me == 0), side[:, columns(group_ref, g, offset)], main[:, here])]
    else:
        parts = [r[:, columns(group_ref, g, offset)] for r in rims]
    return jnp.concatenate([own_ref[:near, here]] + parts, axis=0)


def weight_kernel(small, group_ref, other_ref, q_ref, bias_ref, k_ref, *refs):
    *rims, weight_ref, inverse_ref = refs
    groups, near = q_ref.shape[1] // WIDTH, weight_ref.shape[1] // HEADS_DEV
    q_ref = q_ref.at[pl.ds(0, near)]
    scores = [
        tall_scores(head_stack(q_ref, g), with_rim(k_ref, near, rims, small, (group_ref, other_ref), g, 0), bias_ref[...])
        for g in range(groups)]
    totals = []
    for g in range(groups):
        expo = jnp.exp2(scores[g] - jnp.max(scores[g], axis=0, keepdims=True))
        weight_ref[g] = jnp.transpose(expo.astype(jnp.bfloat16))
        totals.append(jnp.sum(expo, axis=0, keepdims=True))
    spare = inverse_ref.shape[1] - groups
    inverse = 1.0 / jnp.concatenate(totals, axis=0)
    inverse = jnp.concatenate([inverse, jnp.zeros((spare, inverse.shape[1]), jnp.float32)], axis=0) if spare else inverse
    inverse_ref[...] = jnp.transpose(inverse)


def mix_kernel(small, group_ref, other_ref, weight_ref, inverse_ref, v_ref, *refs):
    *rims, out_ref, buf, sem = refs
    groups = weight_ref.shape[0]
    if small:
        *rims, done_ref = rims
        far = pltpu.make_async_copy(done_ref, out_ref.at[pl.ds(buf.shape[0], done_ref.shape[0])], sem.at[groups])
        far.start()
    for g in range(groups):
        value = with_rim(v_ref, buf.shape[0], rims, small, (group_ref, other_ref), g, v_ref.shape[1])
        store_heads(buf, g, mix(weight_ref[g], inverse_ref[:, g:g + 1], value))
        send_out(buf, out_ref, 0, g, sem).start()
    for g in range(groups):
        send_out(buf, out_ref, 0, g, sem).wait()
    if small:
        far.wait()


SMEM = pl.BlockSpec(memory_space=pltpu.SMEM)
VMEM = pl.BlockSpec(memory_space=pltpu.VMEM)
ANY = pl.BlockSpec(memory_space=pl.ANY)


def cycles(devices, period):
    firsts = [0, period // 2 + 1] + [m - 1 for m in range(period, devices, period)] + [devices]
    pairs = []
    for a, b in zip(firsts, firsts[1:]):
        pairs += [(i, i + 1) for i in range(a, b - 1)] + [(b - 1, a)]
    return pairs


def on_device(queries, key_rows, value_rows, group_kv_head, doc_ids):
    rows, width = queries.shape
    devices = lax.axis_size("ctx") * lax.axis_size("head")
    period = 2 * lax.axis_size("head")
    groups = width // WIDTH
    reach = rows * lax.axis_size("head") // 8
    near = min(reach, rows)
    hops = -(-reach // rows)
    small = near < rows
    dtype = queries.dtype
    docs = doc_ids.reshape(devices, rows)
    vmem = lambda x: pltpu.with_memory_space_constraint(x, pltpu.VMEM) if small else x
    chip = pltpu.VMEM if small else jax.ShapeDtypeStruct
    keys = 2 * near if small else rows * (1 + hops)
    kv_shape = key_rows.shape
    sent, early, arguments = {}, [], (group_kv_head, docs, queries, key_rows, value_rows)
    tables = [chip((near, 2 * kv_shape[1]), dtype), chip(docs.shape, jnp.int32), chip(queries.shape, dtype), chip(kv_shape, dtype),
              chip(kv_shape, dtype)]
    names = pltpu.SMEM(group_kv_head.shape, jnp.int32)
    if small:
        key_edge, value_edge, early_group, *early = pl.pallas_call(
            edge_kernel, out_shape=[chip((near, kv_shape[1]), dtype)] * 2 + [names] + tables,
            in_specs=[ANY] * 5, out_specs=[VMEM] * 2 + [SMEM] + [VMEM] * 5, name="edges",
            scratch_shapes=[pltpu.SemaphoreType.DMA((9,))],
        )(*arguments)
        for name, array in (("main_k", key_edge), ("main_v", value_edge)):
            sent[name] = lax.ppermute(array, AXES, cycles(devices, period))
    group, edge, near_docs, q, k, v = pl.pallas_call(
        functools.partial(load_kernel, len(early)), out_shape=[names] + tables,
        in_specs=[ANY] * 5 + [VMEM] * len(early), out_specs=[SMEM] + [VMEM] * 5, name="load",
        scratch_shapes=[pltpu.SemaphoreType.DMA((7,))],
        input_output_aliases={5 + i: 1 + i for i in range(len(early))},
    )(*arguments, *[vmem(x) for x in early])
    groups_of = (group, early_group if small else group)
    bias, *done = pl.pallas_call(
        functools.partial(inner_kernel, near, hops),
        out_shape=[chip((keys, HEADS_DEV * near), jnp.float32)] + [chip((rows - near, width), dtype)] * small,
        in_specs=[SMEM] * 2 + [VMEM] * 4, out_specs=[VMEM] * (1 + small), name="inner",
    )(*groups_of, *[vmem(x) for x in (near_docs, q, k, v)])
    if small:
        side = lax.ppermute(edge, AXES, [(i, i ^ 1) for i in range(devices)])
        key_rims, value_rims = [sent["main_k"], side], [sent["main_v"], side]
    else:
        key_rims = value_rims = [
            lax.ppermute(edge, AXES, [(i, i + j) for i in range(devices - j)]) for j in range(1, hops + 1)]
    stack = HEADS_DEV * near
    weights, inverse = pl.pallas_call(
        functools.partial(weight_kernel, small),
        out_shape=[chip((groups, stack, keys), dtype), chip((stack, -(-groups // 8) * 8), jnp.float32)],
        in_specs=[SMEM] * 2 + [VMEM] * (3 + len(key_rims)), out_specs=[VMEM] * 2, name="weights",
    )(*groups_of, *[vmem(x) for x in (q, bias, k, *key_rims)])
    ins = [vmem(x) for x in (weights, inverse, v, *value_rims, *done)]
    return pl.pallas_call(
        functools.partial(mix_kernel, small),
        out_shape=jax.ShapeDtypeStruct(queries.shape, dtype),
        in_specs=[SMEM] * 2 + [VMEM] * len(ins), out_specs=ANY, name="mix",
        scratch_shapes=[pltpu.VMEM((near, width), dtype), pltpu.SemaphoreType.DMA((groups + 1,))],
    )(*groups_of, *ins)


def solution(mesh):
    placed = P(AXES, None)
    return jax.shard_map(
        on_device, mesh=mesh, in_specs=(placed, placed, placed, P(), P()), out_specs=placed, check_vma=False
    )
```

profile of v0, /device:TPU:8, one launch (start us, length us, event | category | flops | bytes accessed | tf_op | source)
XLA Modules:
  0.0 8.6 jit_solution(2924107828301131919)
XLA Ops:
  0.0 0.1 edges.1
  0.1 1.2 %load.1 = (s32[4]{0:T(128)S(4)}, bf16[64,512]{1,0:T(8,128)(2,1)S(1)}, s32[32,128]{1,0:T(8,128)S(1)}, bf16[128,2048]{1,0:T(8,128)(2,1)S(1)}, bf16[128,256]{1,0:T(8,128)(2,1)S(1)}, /*index=5*/bf16[128,256]{1,0:T(8,128)(2,1)S(1)}) custom-call(s32[4]{0:T(128)} %group_hbm.3, ...), custom_call_target="tpu_custom_call", output_to_operand_aliasing={{1}: (5, {}), {2}: (6, {}), {3}: (7, {}), {4}: (8, {}), {5}... | custom-call | tf_op jit(solution)/shard_map/load/pallas_call | solution.py:240
  1.3 0.7 %collective-permute-start.1 = (bf16[64,512]{1,0:T(8,128)(2,1)S(1)}, bf16[64,512]{1,0:T(8,128)(2,1)S(1)}, u32[]{:S(2)}, u32[]{:S(2)}) collective-permute-start(bf16[64,512]{1,0:T(8,128)(2,1)S(1)} %get-tuple-element.36), channel_id=1, source_target_pairs={{0,1},{1,0},{2,3},{3,2},{4,5},{5,4},{6,7},{7,6},{8,9},{9,8},{10,11... | collective-permute-start | bytes 196616 | tf_op jit(solution)/shard_map/ppermute | solution.py:253
  2.0 0.1 collective-permute-start
  2.1 1.5 %collective-permute-start.2 = (bf16[64,256]{1,0:T(8,128)(2,1)S(1)}, bf16[64,256]{1,0:T(8,128)(2,1)S(1)}, u32[]{:S(2)}, u32[]{:S(2)}) collective-permute-start(bf16[64,256]{1,0:T(8,128)(2,1)S(1)} %get-tuple-element.39), channel_id=1, source_target_pairs={{0,1},{1,2},{2,3},{3,4},{4,0},{5,6},{6,5},{7,8},{8,9},{9,10},{10,1... | collective-permute-start | bytes 98312 | tf_op jit(solution)/shard_map/ppermute | solution.py:239
  3.6 0.8 %inner.1 = (f32[128,256]{1,0:T(8,128)S(1)}, bf16[64,2048]{1,0:T(8,128)(2,1)S(1)}) custom-call(s32[4]{0:T(128)S(4)} %get-tuple-element.28.group_ref, s32[4]{0:T(128)S(4)} %get-tuple-element.29.other_ref, s32[32,128]{1,0:T(8,128)S(1)} %get-tuple-element.31.doc_ref, bf16[128,2048]{1,0:T(8,128)(2,1)S(1)} %get-tuple-element.30.q_ref, ...), custom_call_target="tpu_custom_call" | custom-call | tf_op jit(solution)/shard_map/inner/pallas_call | solution.py:247
  4.4 2.8 %collective-permute-done.refs_0_ = bf16[64,256]{1,0:T(8,128)(2,1)S(1)} collective-permute-done((bf16[64,256]{1,0:T(8,128)(2,1)S(1)}, bf16[64,256]{1,0:T(8,128)(2,1)S(1)}, u32[]{:S(2)}, u32[]{:S(2)}) %collective-permute-start) | collective-permute-done | bytes 32800 | tf_op jit(solution)/shard_map/ppermute | solution.py:239
  7.1 0.0 collective-permute-done.1.refs_1_
  7.2 0.4 %weights.1 = (bf16[4,256,128]{2,1,0:T(8,128)(2,1)S(1)}, f32[256,8]{1,0:T(8,128)S(1)}) custom-call(s32[4]{0:T(128)S(4)} %get-tuple-element.28.group_ref, s32[4]{0:T(128)S(4)} %get-tuple-element.29.other_ref, bf16[128,2048]{1,0:T(8,128)(2,1)S(1)} %get-tuple-element.30.q_ref, f32[128,256]{1,0:T(8,128)S(1)} %get-tuple-element.34.bias_ref, ...), custom_call_target="tpu_custom_call" | custom-call | tf_op jit(solution)/shard_map/weights/pallas_call | solution.py:259
  7.6 0.0 collective-permute-done.2.refs_0_
  7.6 0.9 %mix.1 = bf16[128,2048]{1,0:T(8,128)(2,1)} custom-call(s32[4]{0:T(128)S(4)} %get-tuple-element.28.group_ref, s32[4]{0:T(128)S(4)} %get-tuple-element.29.other_ref, bf16[4,256,128]{2,1,0:T(8,128)(2,1)S(1)} %get-tuple-element.37.weight_ref, f32[256,8]{1,0:T(8,128)S(1)} %get-tuple-element.38.inverse_ref, bf16[128,256]{1,0:T(8,128)(2,1)S(1)} %get-tuple-element.33.v_ref, ...), custom_call_target="tpu_custom_call" | custom-call | tf_op jit(solution)/shard_map/mix/pallas_call | solution.py:265
Async XLA Ops:
  1.3 5.8 %collective-permute-start.1 = (bf16[64,512]{1,0:T(8,128)(2,1)S(1)}, bf16[64,512]{1,0:T(8,128)(2,1)S(1)}, u32[]{:S(2)}, u32[]{:S(2)}) collective-permute-start(bf16[64,512]{1,0:T(8,128)(2,1)S(1)} %get-tuple-element.36), channel_id=1, source_target_pairs={{0,1},{1,0},{2,3},{3,2},{4,5},{5,4},{6,7},{7,6},{8,9},{9,8},{10,11... | collective-permute-start | bytes 196616 | tf_op jit(solution)/shard_map/ppermute | solution.py:253
  2.0 5.1 %collective-permute-start = (bf16[64,256]{1,0:T(8,128)(2,1)S(1)}, bf16[64,256]{1,0:T(8,128)(2,1)S(1)}, u32[]{:S(2)}, u32[]{:S(2)}) collective-permute-start(bf16[64,256]{1,0:T(8,128)(2,1)S(1)} %get-tuple-element.35), channel_id=1, source_target_pairs={{0,1},{1,2},{2,3},{3,4},{4,0},{5,6},{6,5},{7,8},{8,9},{9,10},{10,1... | collective-permute-start | bytes 98312 | tf_op jit(solution)/shard_map/ppermute | solution.py:239
  2.1 5.5 %collective-permute-start.2 = (bf16[64,256]{1,0:T(8,128)(2,1)S(1)}, bf16[64,256]{1,0:T(8,128)(2,1)S(1)}, u32[]{:S(2)}, u32[]{:S(2)}) collective-permute-start(bf16[64,256]{1,0:T(8,128)(2,1)S(1)} %get-tuple-element.39), channel_id=1, source_target_pairs={{0,1},{1,2},{2,3},{3,4},{4,0},{5,6},{6,5},{7,8},{8,9},{9,10},{10,1... | collective-permute-start | bytes 98312 | tf_op jit(solution)/shard_map/ppermute | solution.py:239
where the time goes:
time: 8.71 us; the launch traced here: 8.56 us
  Pallas kernels  3.47 us (40%)
  waiting for transfers between devices  2.77 us (32%)
  starting transfers between devices  2.28 us (26%)
    ppermute x2, waiting for transfers between devices, on_device(): sent[name] = lax.ppermute(array, AXES, cycles(devices, period))  2.76 us
    ppermute x2, starting transfers between devices, on_device(): sent[name] = lax.ppermute(array, AXES, cycles(devices, period))  1.61 us
    pallas_call x1, Pallas kernels, on_device(): pl.pallas_call(functools.partial(load_kernel, len(early)), out_shape=[nam...  1.24 us
    pallas_call x1, Pallas kernels, on_device(): pl.pallas_call(functools.partial(mix_kernel, small), out_shape=jax.ShapeD...  0.95 us
    pallas_call x1, Pallas kernels, on_device(): pl.pallas_call(functools.partial(inner_kernel, near, hops), out_shape=[ch...  0.76 us
    ppermute x1, starting transfers between devices, on_device(): side = lax.ppermute(edge, AXES, [(i, i ^ 1) for i in range(devices)])  0.67 us
    pallas_call x1, Pallas kernels, on_device(): pl.pallas_call(functools.partial(weight_kernel, small), out_shape=[chip((...  0.44 us
  transfers between devices with their start and end apart: 3, of which 1 were waited for; matrix products, arithmetic and copies ran while one was open for 0% of the time, Pallas kernels for 14%

commit v1 on v0

--- a/solution.py
+++ b/solution.py
@@ -86,16 +86,21 @@
     return hbm.at[pl.ds(hbm.shape[0] - near, near)]
 
 
-def own_loads(doc_hbm, q_hbm, k_hbm, v_hbm, edge_ref, doc_ref, q_ref, k_ref, v_ref):
+def edge_loads(k_hbm, v_hbm, edge_ref):
     near, width = edge_ref.shape[0], k_hbm.shape[1]
-    return [(last_rows(k_hbm, near), edge_ref.at[:, pl.ds(0, width)]), (last_rows(v_hbm, near), edge_ref.at[:, pl.ds(width, width)]),
-            (doc_hbm, doc_ref), (k_hbm, k_ref), (v_hbm, v_ref), (q_hbm, q_ref)]
+    return [(last_rows(k_hbm, near), edge_ref.at[:, pl.ds(0, width)]), (last_rows(v_hbm, near), edge_ref.at[:, pl.ds(width, width)])]
+
+
+def own_loads(doc_hbm, q_hbm, k_hbm, v_hbm, doc_ref, q_ref, k_ref, v_ref):
+    return [(doc_hbm, doc_ref), (k_hbm, k_ref), (v_hbm, v_ref), (q_hbm, q_ref)]
 
 
 def edge_kernel(group_hbm, doc_hbm, q_hbm, k_hbm, v_hbm, key_ref, value_ref, group_ref, *refs):
     *refs, sem = refs
-    near = key_ref.shape[0]
-    pairs = [(last_rows(k_hbm, near), key_ref), (last_rows(v_hbm, near), value_ref)]
+    extra = (key_ref.shape[0] - value_ref.shape[0]) // 2
+    near, rest = key_ref.shape[0] - extra, value_ref.shape[0]
+    pairs = [(last_rows(k_hbm, near), key_ref.at[pl.ds(0, near)]), (last_rows(v_hbm, rest), value_ref),
+             (v_hbm.at[pl.ds(v_hbm.shape[0] - near, extra)], key_ref.at[pl.ds(near, extra)])]
 
     me = flat_index()
 
@@ -107,22 +112,27 @@
 
         @pl.when(first_pair())
         def _():
-            run_all([(group_hbm, group_ref)] + own_loads(doc_hbm, q_hbm, k_hbm, v_hbm, *refs), sem.at[pl.ds(len(pairs), 7)])
+            run_all([(group_hbm, group_ref)] + own_loads(doc_hbm, q_hbm, k_hbm, v_hbm, *refs), sem.at[pl.ds(len(pairs), 5)])
 
         for copy in copies:
             copy.wait()
 
 
 def load_kernel(given, group_hbm, doc_hbm, q_hbm, k_hbm, v_hbm, *refs):
-    group_ref, *refs, sem = refs[given:]
+    edge_ref, group_ref, *refs, sem = refs[given:]
     loads = [(group_hbm, group_ref)] + own_loads(doc_hbm, q_hbm, k_hbm, v_hbm, *refs)
     if not given:
-        run_all(loads, sem)
+        run_all(edge_loads(k_hbm, v_hbm, edge_ref) + loads, sem)
         return
+
+    @pl.when(first_pair())
+    def _():
+        edge_ref[:, :k_hbm.shape[1]] = refs[2][refs[2].shape[0] - edge_ref.shape[0]:]
+        edge_ref[:, k_hbm.shape[1]:] = refs[3][refs[3].shape[0] - edge_ref.shape[0]:]
 
     @pl.when(jnp.logical_not(first_pair()))
     def _():
-        run_all(loads, sem)
+        run_all(edge_loads(k_hbm, v_hbm, edge_ref) + loads, sem)
 
 
 def inner_kernel(near, hops, group_ref, other_ref, doc_ref, q_ref, k_ref, v_ref, bias_ref, *out_ref):
@@ -155,8 +165,12 @@
     here = columns(group_ref, g)
     if small:
         me = flat_index()
-        main, side = rims
-        parts = [jnp.where((me % 2 == 1) | (me == 0), side[:, columns(group_ref, g, offset)], main[:, here])]
+        *main, side = rims
+        if offset:
+            main = jnp.concatenate([main[0][near:, here], main[1][:, here]], axis=0)
+        else:
+            main = main[0][:near, here]
+        parts = [jnp.where((me % 2 == 1) | (me == 0), side[:, columns(group_ref, g, offset)], main)]
     else:
         parts = [r[:, columns(group_ref, g, offset)] for r in rims]
     return jnp.concatenate([own_ref[:near, here]] + parts, axis=0)
@@ -226,22 +240,23 @@
     keys = 2 * near if small else rows * (1 + hops)
     kv_shape = key_rows.shape
     sent, early, arguments = {}, [], (group_kv_head, docs, queries, key_rows, value_rows)
-    tables = [chip((near, 2 * kv_shape[1]), dtype), chip(docs.shape, jnp.int32), chip(queries.shape, dtype), chip(kv_shape, dtype),
-              chip(kv_shape, dtype)]
+    tables = [chip(docs.shape, jnp.int32), chip(queries.shape, dtype), chip(kv_shape, dtype), chip(kv_shape, dtype)]
     names = pltpu.SMEM(group_kv_head.shape, jnp.int32)
     if small:
+        extra = near // 4
         key_edge, value_edge, early_group, *early = pl.pallas_call(
-            edge_kernel, out_shape=[chip((near, kv_shape[1]), dtype)] * 2 + [names] + tables,
-            in_specs=[ANY] * 5, out_specs=[VMEM] * 2 + [SMEM] + [VMEM] * 5, name="edges",
-            scratch_shapes=[pltpu.SemaphoreType.DMA((9,))],
+            edge_kernel,
+            out_shape=[chip((near + extra, kv_shape[1]), dtype), chip((near - extra, kv_shape[1]), dtype), names] + tables,
+            in_specs=[ANY] * 5, out_specs=[VMEM] * 2 + [SMEM] + [VMEM] * 4, name="edges",
+            scratch_shapes=[pltpu.SemaphoreType.DMA((8,))],
         )(*arguments)
         for name, array in (("main_k", key_edge), ("main_v", value_edge)):
             sent[name] = lax.ppermute(array, AXES, cycles(devices, period))
-    group, edge, near_docs, q, k, v = pl.pallas_call(
-        functools.partial(load_kernel, len(early)), out_shape=[names] + tables,
-        in_specs=[ANY] * 5 + [VMEM] * len(early), out_specs=[SMEM] + [VMEM] * 5, name="load",
+    edge, group, near_docs, q, k, v = pl.pallas_call(
+        functools.partial(load_kernel, len(early)), out_shape=[chip((near, 2 * kv_shape[1]), dtype), names] + tables,
+        in_specs=[ANY] * 5 + [VMEM] * len(early), out_specs=[VMEM, SMEM] + [VMEM] * 4, name="load",
         scratch_shapes=[pltpu.SemaphoreType.DMA((7,))],
-        input_output_aliases={5 + i: 1 + i for i in range(len(early))},
+        input_output_aliases={5 + i: 2 + i for i in range(len(early))},
     )(*arguments, *[vmem(x) for x in early])
     groups_of = (group, early_group if small else group)
     bias, *done = pl.pallas_call(
@@ -251,7 +266,7 @@
     )(*groups_of, *[vmem(x) for x in (near_docs, q, k, v)])
     if small:
         side = lax.ppermute(edge, AXES, [(i, i ^ 1) for i in range(devices)])
-        key_rims, value_rims = [sent["main_k"], side], [sent["main_v"], side]
+        key_rims, value_rims = [sent["main_k"], side], [sent["main_k"], sent["main_v"], side]
     else:
         key_rims = value_rims = [
             lax.ppermute(edge, AXES, [(i, i + j) for i in range(devices - j)]) for j in range(1, hops + 1)]

time: 8.71 us -> 8.78 us (level)
  the two profiles are of different devices: /device:TPU:8 before, /device:TPU:16 now
where the time goes in v1:
time: 8.78 us; the launch traced here: 8.63 us
  Pallas kernels  3.47 us (40%)
  waiting for transfers between devices  2.85 us (32%)
  starting transfers between devices  2.27 us (26%)
    ppermute x2, waiting for transfers between devices, on_device(): sent[name] = lax.ppermute(array, AXES, cycles(devices, period))  2.85 us
    ppermute x2, starting transfers between devices, on_device(): sent[name] = lax.ppermute(array, AXES, cycles(devices, period))  1.61 us
    pallas_call x1, Pallas kernels, on_device(): pl.pallas_call(functools.partial(load_kernel, len(early)), out_shape=[chi...  1.24 us
    pallas_call x1, Pallas kernels, on_device(): pl.pallas_call(functools.partial(mix_kernel, small), out_shape=jax.ShapeD...  0.95 us
    pallas_call x1, Pallas kernels, on_device(): pl.pallas_call(functools.partial(inner_kernel, near, hops), out_shape=[ch...  0.76 us
    ppermute x1, starting transfers between devices, on_device(): side = lax.ppermute(edge, AXES, [(i, i ^ 1) for i in range(devices)])  0.66 us
    pallas_call x1, Pallas kernels, on_device(): pl.pallas_call(functools.partial(weight_kernel, small), out_shape=[chip((...  0.44 us
  transfers between devices with their start and end apart: 3, of which 1 were waited for; matrix products, arithmetic and copies ran while one was open for 0% of the time, Pallas kernels for 14%

profile of v1, /device:TPU:16, one launch (start us, length us, event | category | flops | bytes accessed | tf_op | source)
XLA Modules:
  0.0 8.6 jit_solution(5012955260353614677)
XLA Ops:
  0.0 0.1 edges.1
  0.1 1.2 %load.1 = (bf16[64,512]{1,0:T(8,128)(2,1)S(1)}, s32[4]{0:T(128)S(4)}, s32[32,128]{1,0:T(8,128)S(1)}, bf16[128,2048]{1,0:T(8,128)(2,1)S(1)}, bf16[128,256]{1,0:T(8,128)(2,1)S(1)}, /*index=5*/bf16[128,256]{1,0:T(8,128)(2,1)S(1)}) custom-call(s32[4]{0:T(128)} %group_hbm.3, ...), custom_call_target="tpu_custom_call", output_to_operand_aliasing={{2}: (5, {}), {3}: (6, {}), {4}: (7, {}), {5}: (8, {})} | custom-call | tf_op jit(solution)/shard_map/load/pallas_call | solution.py:255
  1.3 0.7 %collective-permute-start.1 = (bf16[64,512]{1,0:T(8,128)(2,1)S(1)}, bf16[64,512]{1,0:T(8,128)(2,1)S(1)}, u32[]{:S(2)}, u32[]{:S(2)}) collective-permute-start(bf16[64,512]{1,0:T(8,128)(2,1)S(1)} %get-tuple-element.34), channel_id=1, source_target_pairs={{0,1},{1,0},{2,3},{3,2},{4,5},{5,4},{6,7},{7,6},{8,9},{9,8},{10,11... | collective-permute-start | bytes 196616 | tf_op jit(solution)/shard_map/ppermute | solution.py:268
  2.0 0.1 collective-permute-start
  2.1 1.5 %collective-permute-start.2 = (bf16[48,256]{1,0:T(8,128)(2,1)S(1)}, bf16[48,256]{1,0:T(8,128)(2,1)S(1)}, u32[]{:S(2)}, u32[]{:S(2)}) collective-permute-start(bf16[48,256]{1,0:T(8,128)(2,1)S(1)} %get-tuple-element.37), channel_id=1, source_target_pairs={{0,1},{1,2},{2,3},{3,4},{4,0},{5,6},{6,5},{7,8},{8,9},{9,10},{10,1... | collective-permute-start | bytes 73736 | tf_op jit(solution)/shard_map/ppermute | solution.py:254
  3.6 0.8 %inner.1 = (f32[128,256]{1,0:T(8,128)S(1)}, bf16[64,2048]{1,0:T(8,128)(2,1)S(1)}) custom-call(s32[4]{0:T(128)S(4)} %get-tuple-element.26.group_ref, s32[4]{0:T(128)S(4)} %get-tuple-element.27.other_ref, s32[32,128]{1,0:T(8,128)S(1)} %get-tuple-element.29.doc_ref, bf16[128,2048]{1,0:T(8,128)(2,1)S(1)} %get-tuple-element.28.q_ref, ...), custom_call_target="tpu_custom_call" | custom-call | tf_op jit(solution)/shard_map/inner/pallas_call | solution.py:262
  4.4 2.8 %collective-permute-done.refs_0_ = bf16[80,256]{1,0:T(8,128)(2,1)S(1)} collective-permute-done((bf16[80,256]{1,0:T(8,128)(2,1)S(1)}, bf16[80,256]{1,0:T(8,128)(2,1)S(1)}, u32[]{:S(2)}, u32[]{:S(2)}) %collective-permute-start) | collective-permute-done | bytes 40992 | tf_op jit(solution)/shard_map/ppermute | solution.py:254
  7.2 0.0 collective-permute-done.1.refs_1_.refs_2_
  7.2 0.4 %weights.1 = (bf16[4,256,128]{2,1,0:T(8,128)(2,1)S(1)}, f32[256,8]{1,0:T(8,128)S(1)}) custom-call(s32[4]{0:T(128)S(4)} %get-tuple-element.26.group_ref, s32[4]{0:T(128)S(4)} %get-tuple-element.27.other_ref, bf16[128,2048]{1,0:T(8,128)(2,1)S(1)} %get-tuple-element.28.q_ref, f32[128,256]{1,0:T(8,128)S(1)} %get-tuple-element.32.bias_ref, ...), custom_call_target="tpu_custom_call" | custom-call | tf_op jit(solution)/shard_map/weights/pallas_call | solution.py:274
  7.7 0.0 collective-permute-done.2.refs_1_
  7.7 1.0 %mix.1 = bf16[128,2048]{1,0:T(8,128)(2,1)} custom-call(s32[4]{0:T(128)S(4)} %get-tuple-element.26.group_ref, s32[4]{0:T(128)S(4)} %get-tuple-element.27.other_ref, bf16[4,256,128]{2,1,0:T(8,128)(2,1)S(1)} %get-tuple-element.35.weight_ref, f32[256,8]{1,0:T(8,128)S(1)} %get-tuple-element.36.inverse_ref, bf16[128,256]{1,0:T(8,128)(2,1)S(1)} %get-tuple-element.31.v_ref, ...), custom_call_target="tpu_custom_call" | custom-call | tf_op jit(solution)/shard_map/mix/pallas_call | solution.py:280
Async XLA Ops:
  1.3 5.9 %collective-permute-start.1 = (bf16[64,512]{1,0:T(8,128)(2,1)S(1)}, bf16[64,512]{1,0:T(8,128)(2,1)S(1)}, u32[]{:S(2)}, u32[]{:S(2)}) collective-permute-start(bf16[64,512]{1,0:T(8,128)(2,1)S(1)} %get-tuple-element.34), channel_id=1, source_target_pairs={{0,1},{1,0},{2,3},{3,2},{4,5},{5,4},{6,7},{7,6},{8,9},{9,8},{10,11... | collective-permute-start | bytes 196616 | tf_op jit(solution)/shard_map/ppermute | solution.py:268
  2.0 5.2 %collective-permute-start = (bf16[80,256]{1,0:T(8,128)(2,1)S(1)}, bf16[80,256]{1,0:T(8,128)(2,1)S(1)}, u32[]{:S(2)}, u32[]{:S(2)}) collective-permute-start(bf16[80,256]{1,0:T(8,128)(2,1)S(1)} %get-tuple-element.33), channel_id=1, source_target_pairs={{0,1},{1,2},{2,3},{3,4},{4,0},{5,6},{6,5},{7,8},{8,9},{9,10},{10,1... | collective-permute-start | bytes 122888 | tf_op jit(solution)/shard_map/ppermute | solution.py:254
  2.1 5.6 %collective-permute-start.2 = (bf16[48,256]{1,0:T(8,128)(2,1)S(1)}, bf16[48,256]{1,0:T(8,128)(2,1)S(1)}, u32[]{:S(2)}, u32[]{:S(2)}) collective-permute-start(bf16[48,256]{1,0:T(8,128)(2,1)S(1)} %get-tuple-element.37), channel_id=1, source_target_pairs={{0,1},{1,2},{2,3},{3,4},{4,0},{5,6},{6,5},{7,8},{8,9},{9,10},{10,1... | collective-permute-start | bytes 73736 | tf_op jit(solution)/shard_map/ppermute | solution.py:254

commit v2 on v1

--- a/solution.py
+++ b/solution.py
@@ -135,7 +135,7 @@
         run_all(edge_loads(k_hbm, v_hbm, edge_ref) + loads, sem)
 
 
-def inner_kernel(near, hops, group_ref, other_ref, doc_ref, q_ref, k_ref, v_ref, bias_ref, *out_ref):
+def inner_kernel(near, hops, group_ref, other_ref, doc_ref, q_ref, k_ref, v_ref, bias_ref, local_ref, *out_ref):
     rows, width = q_ref.shape
     me = flat_index()
     own = doc_ref[pl.ds(me, 1), :]
@@ -151,7 +151,11 @@
         docs = column_of(jnp.where(lax.broadcasted_iota(jnp.int32, own.shape, 1) < near, own, before[0]))
         pos = jnp.where(t < near, t, t - rows)
         seen = [bias_of((docs == own) & (pos <= u) & (pos + me * rows >= 0))[:, :near]]
-    bias_ref[...] = jnp.concatenate([jnp.concatenate(seen, axis=0)] * HEADS_DEV, axis=1)
+    tall = jnp.concatenate([jnp.concatenate(seen, axis=0)] * HEADS_DEV, axis=1)
+    bias_ref[...] = tall[near:]
+    first = q_ref.at[pl.ds(0, near)]
+    for g in range(width // WIDTH):
+        local_ref[g] = tall_scores(head_stack(first, g), k_ref[:near, columns((group_ref, other_ref), g)], tall[:near])
     if near < rows:
         bias = bias_of((own == col) & (u <= t))[near:]
         far = q_ref.at[pl.ds(near, rows - near)]
@@ -173,16 +177,16 @@
         parts = [jnp.where((me % 2 == 1) | (me == 0), side[:, columns(group_ref, g, offset)], main)]
     else:
         parts = [r[:, columns(group_ref, g, offset)] for r in rims]
-    return jnp.concatenate([own_ref[:near, here]] + parts, axis=0)
-
-
-def weight_kernel(small, group_ref, other_ref, q_ref, bias_ref, k_ref, *refs):
+    return jnp.concatenate(([] if own_ref is None else [own_ref[:near, here]]) + parts, axis=0)
+
+
+def weight_kernel(small, group_ref, other_ref, q_ref, bias_ref, local_ref, *refs):
     *rims, weight_ref, inverse_ref = refs
     groups, near = q_ref.shape[1] // WIDTH, weight_ref.shape[1] // HEADS_DEV
     q_ref = q_ref.at[pl.ds(0, near)]
-    scores = [
-        tall_scores(head_stack(q_ref, g), with_rim(k_ref, near, rims, small, (group_ref, other_ref), g, 0), bias_ref[...])
-        for g in range(groups)]
+    rims = [with_rim(None, near, rims, small, (group_ref, other_ref), g, 0) for g in range(groups)]
+    scores = [tall_scores(head_stack(q_ref, g), rims[g], bias_ref[...]) for g in range(groups)]
+    scores = [jnp.concatenate([local_ref[g], scores[g]], axis=0) for g in range(groups)]
     totals = []
     for g in range(groups):
         expo = jnp.exp2(scores[g] - jnp.max(scores[g], axis=0, keepdims=True))
@@ -259,10 +263,11 @@
         input_output_aliases={5 + i: 2 + i for i in range(len(early))},
     )(*arguments, *[vmem(x) for x in early])
     groups_of = (group, early_group if small else group)
-    bias, *done = pl.pallas_call(
+    bias, local, *done = pl.pallas_call(
         functools.partial(inner_kernel, near, hops),
-        out_shape=[chip((keys, HEADS_DEV * near), jnp.float32)] + [chip((rows - near, width), dtype)] * small,
-        in_specs=[SMEM] * 2 + [VMEM] * 4, out_specs=[VMEM] * (1 + small), name="inner",
+        out_shape=[chip((keys - near, HEADS_DEV * near), jnp.float32), chip((groups, near, HEADS_DEV * near), jnp.float32)]
+        + [chip((rows - near, width), dtype)] * small,
+        in_specs=[SMEM] * 2 + [VMEM] * 4, out_specs=[VMEM] * (2 + small), name="inner",
     )(*groups_of, *[vmem(x) for x in (near_docs, q, k, v)])
     if small:
         side = lax.ppermute(edge, AXES, [(i, i ^ 1) for i in range(devices)])
@@ -275,7 +280,7 @@
         functools.partial(weight_kernel, small),
         out_shape=[chip((groups, stack, keys), dtype), chip((stack, -(-groups // 8) * 8), jnp.float32)],
         in_specs=[SMEM] * 2 + [VMEM] * (3 + len(key_rims)), out_specs=[VMEM] * 2, name="weights",
-    )(*groups_of, *[vmem(x) for x in (q, bias, k, *key_rims)])
+    )(*groups_of, *[vmem(x) for x in (q, bias, local, *key_rims)])
     ins = [vmem(x) for x in (weights, inverse, v, *value_rims, *done)]
     return pl.pallas_call(
         functools.partial(mix_kernel, small),

time: 8.78 us -> 8.76 us (level)
  the two profiles are of different devices: /device:TPU:16 before, /device:TPU:24 now
where the time goes in v2:
time: 8.76 us; the launch traced here: 8.61 us
  Pallas kernels  3.52 us (40%)
  waiting for transfers between devices  2.78 us (32%)
  starting transfers between devices  2.27 us (26%)
    ppermute x2, waiting for transfers between devices, on_device(): sent[name] = lax.ppermute(array, AXES, cycles(devices, period))  2.78 us
    ppermute x2, starting transfers between devices, on_device(): sent[name] = lax.ppermute(array, AXES, cycles(devices, period))  1.61 us
    pallas_call x1, Pallas kernels, on_device(): pl.pallas_call(functools.partial(load_kernel, len(early)), out_shape=[chi...  1.24 us
    pallas_call x1, Pallas kernels, on_device(): pl.pallas_call(functools.partial(mix_kernel, small), out_shape=jax.ShapeD...  0.95 us
    pallas_call x1, Pallas kernels, on_device(): pl.pallas_call(functools.partial(inner_kernel, near, hops), out_shape=[ch...  0.83 us
    ppermute x1, starting transfers between devices, on_device(): side = lax.ppermute(edge, AXES, [(i, i ^ 1) for i in range(devices)])  0.66 us
    pallas_call x1, Pallas kernels, on_device(): pl.pallas_call(functools.partial(weight_kernel, small), out_shape=[chip((...  0.42 us
  transfers between devices with their start and end apart: 3, of which 1 were waited for; matrix products, arithmetic and copies ran while one was open for 0% of the time, Pallas kernels for 15%

profile of v2, /device:TPU:24, one launch (start us, length us, event | category | flops | bytes accessed | tf_op | source)
XLA Modules:
  0.0 8.6 jit_solution(9997572490661342158)
XLA Ops:
  0.0 0.1 edges.1
  0.1 1.2 %load.1 = (bf16[64,512]{1,0:T(8,128)(2,1)S(1)}, s32[4]{0:T(128)S(4)}, s32[32,128]{1,0:T(8,128)S(1)}, bf16[128,2048]{1,0:T(8,128)(2,1)S(1)}, bf16[128,256]{1,0:T(8,128)(2,1)S(1)}, /*index=5*/bf16[128,256]{1,0:T(8,128)(2,1)S(1)}) custom-call(s32[4]{0:T(128)} %group_hbm.3, ...), custom_call_target="tpu_custom_call", output_to_operand_aliasing={{2}: (5, {}), {3}: (6, {}), {4}: (7, {}), {5}: (8, {})} | custom-call | tf_op jit(solution)/shard_map/load/pallas_call | solution.py:259
  1.3 0.7 %collective-permute-start.1 = (bf16[64,512]{1,0:T(8,128)(2,1)S(1)}, bf16[64,512]{1,0:T(8,128)(2,1)S(1)}, u32[]{:S(2)}, u32[]{:S(2)}) collective-permute-start(bf16[64,512]{1,0:T(8,128)(2,1)S(1)} %get-tuple-element.36), channel_id=1, source_target_pairs={{0,1},{1,0},{2,3},{3,2},{4,5},{5,4},{6,7},{7,6},{8,9},{9,8},{10,11... | collective-permute-start | bytes 196616 | tf_op jit(solution)/shard_map/ppermute | solution.py:273
  2.0 0.1 collective-permute-start
  2.1 1.5 %collective-permute-start.2 = (bf16[48,256]{1,0:T(8,128)(2,1)S(1)}, bf16[48,256]{1,0:T(8,128)(2,1)S(1)}, u32[]{:S(2)}, u32[]{:S(2)}) collective-permute-start(bf16[48,256]{1,0:T(8,128)(2,1)S(1)} %get-tuple-element.39), channel_id=1, source_target_pairs={{0,1},{1,2},{2,3},{3,4},{4,0},{5,6},{6,5},{7,8},{8,9},{9,10},{10,1... | collective-permute-start | bytes 73736 | tf_op jit(solution)/shard_map/ppermute | solution.py:258
  3.6 0.8 %inner.1 = (f32[64,256]{1,0:T(8,128)S(1)}, f32[4,64,256]{2,1,0:T(8,128)S(1)}, bf16[64,2048]{1,0:T(8,128)(2,1)S(1)}) custom-call(s32[4]{0:T(128)S(4)} %get-tuple-element.27.group_ref, s32[4]{0:T(128)S(4)} %get-tuple-element.28.other_ref, s32[32,128]{1,0:T(8,128)S(1)} %get-tuple-element.30.doc_ref, bf16[128,2048]{1,0:T(8,128)(2,1)S(1)} %get-tuple-element.29.q_ref, ...), custom_call_target="tpu_custom_call" | custom-call | tf_op jit(solution)/shard_map/inner/pallas_call | solution.py:266
  4.4 2.8 %collective-permute-done.refs_0_ = bf16[80,256]{1,0:T(8,128)(2,1)S(1)} collective-permute-done((bf16[80,256]{1,0:T(8,128)(2,1)S(1)}, bf16[80,256]{1,0:T(8,128)(2,1)S(1)}, u32[]{:S(2)}, u32[]{:S(2)}) %collective-permute-start) | collective-permute-done | bytes 40992 | tf_op jit(solution)/shard_map/ppermute | solution.py:258
  7.2 0.0 collective-permute-done.1.refs_1_.refs_2_
  7.2 0.4 %weights.1 = (bf16[4,256,128]{2,1,0:T(8,128)(2,1)S(1)}, f32[256,8]{1,0:T(8,128)S(1)}) custom-call(s32[4]{0:T(128)S(4)} %get-tuple-element.27.group_ref, s32[4]{0:T(128)S(4)} %get-tuple-element.28.other_ref, bf16[128,2048]{1,0:T(8,128)(2,1)S(1)} %get-tuple-element.29.q_ref, f32[64,256]{1,0:T(8,128)S(1)} %get-tuple-element.33.bias_ref, ...), custom_call_target="tpu_custom_call" | custom-call | tf_op jit(solution)/shard_map/weights/pallas_call | solution.py:279
  7.6 0.0 collective-permute-done.2.refs_1_
  7.7 1.0 %mix.1 = bf16[128,2048]{1,0:T(8,128)(2,1)} custom-call(s32[4]{0:T(128)S(4)} %get-tuple-element.27.group_ref, s32[4]{0:T(128)S(4)} %get-tuple-element.28.other_ref, bf16[4,256,128]{2,1,0:T(8,128)(2,1)S(1)} %get-tuple-element.37.weight_ref, f32[256,8]{1,0:T(8,128)S(1)} %get-tuple-element.38.inverse_ref, bf16[128,256]{1,0:T(8,128)(2,1)S(1)} %get-tuple-element.32.v_ref, ...), custom_call_target="tpu_custom_call" | custom-call | tf_op jit(solution)/shard_map/mix/pallas_call | solution.py:285
Async XLA Ops:
  1.3 5.9 %collective-permute-start.1 = (bf16[64,512]{1,0:T(8,128)(2,1)S(1)}, bf16[64,512]{1,0:T(8,128)(2,1)S(1)}, u32[]{:S(2)}, u32[]{:S(2)}) collective-permute-start(bf16[64,512]{1,0:T(8,128)(2,1)S(1)} %get-tuple-element.36), channel_id=1, source_target_pairs={{0,1},{1,0},{2,3},{3,2},{4,5},{5,4},{6,7},{7,6},{8,9},{9,8},{10,11... | collective-permute-start | bytes 196616 | tf_op jit(solution)/shard_map/ppermute | solution.py:273
  2.0 5.2 %collective-permute-start = (bf16[80,256]{1,0:T(8,128)(2,1)S(1)}, bf16[80,256]{1,0:T(8,128)(2,1)S(1)}, u32[]{:S(2)}, u32[]{:S(2)}) collective-permute-start(bf16[80,256]{1,0:T(8,128)(2,1)S(1)} %get-tuple-element.35), channel_id=1, source_target_pairs={{0,1},{1,2},{2,3},{3,4},{4,0},{5,6},{6,5},{7,8},{8,9},{9,10},{10,1... | collective-permute-start | bytes 122888 | tf_op jit(solution)/shard_map/ppermute | solution.py:258
  2.1 5.6 %collective-permute-start.2 = (bf16[48,256]{1,0:T(8,128)(2,1)S(1)}, bf16[48,256]{1,0:T(8,128)(2,1)S(1)}, u32[]{:S(2)}, u32[]{:S(2)}) collective-permute-start(bf16[48,256]{1,0:T(8,128)(2,1)S(1)} %get-tuple-element.39), channel_id=1, source_target_pairs={{0,1},{1,2},{2,3},{3,4},{4,0},{5,6},{6,5},{7,8},{8,9},{9,10},{10,1... | collective-permute-start | bytes 73736 | tf_op jit(solution)/shard_map/ppermute | solution.py:258
